TPU v7x, 32 devices: a whole 2x2x4 slice. The times are simulated.
32 devices in a mesh: tm: 16 (over z, y, x), replay: 2 (over core).
Axes of the slice: x: 2, y: 2, z: 4, core: 2. Of those that a mesh axis runs over, the one named last changes fastest.
Arguments:
- obs_store: float32 [2, 1024, 64], P('replay', 'tm'), may hold values from -240 to 240
- observed: int32 [2048], P(('tm', 'replay')), may hold values 0 or 1
- transition: float32 [128, 128], replicated, may hold values from -1 to 1, as said below
- obs_map: float32 [64, 128], replicated, may hold values from -0.5 to 0.5
- gain_weights: float32 [64], replicated, may hold values from 0.00048828125 to 0.009765625
- init_mean: float32 [128], replicated, may hold values from -6 to 6
- smoothed_cov: float32 [128, 128], replicated, may hold values from -0.01 to 0.8, as said below
Outputs:
- smoothed: float32 [2048, 128], P(('tm', 'replay'))
- new_transition: float32 [128, 128], replicated
Inputs may be any that keep to these rules, and one draw needn't show every extreme that they name: `transition`: its spectral norm is below 1. `smoothed_cov`: symmetric positive definite.
All inputs are finite; a program needn't handle non-finite values. No bound on the sum of `observed` on one device may be relied on, other than what follows from the above.
Results may differ from a plain program's by a relative error of at most 0.0003.
Values sent between devices are 32-bit elements; how exact they have to be, the bound alone decides.
A program may use at most 128 MiB of HBM per device.

v0:
```python
import functools

import jax
import jax.numpy as jnp
from jax import lax
from jax.experimental import pallas as pl
from jax.experimental.pallas import tpu as pltpu
from jax.sharding import PartitionSpec as P

MESH = pl.DeviceIdType.MESH
F32 = jnp.float32


def mm(a, b):
    return jnp.dot(a, b, precision=lax.Precision.HIGHEST, preferred_element_type=F32)


def halves(a):
    high = a.astype(jnp.bfloat16)
    return high, (a - high.astype(F32)).astype(jnp.bfloat16)


def mm_apply(a, b):
    rows = a.shape[0]
    a_high, a_low = halves(a)
    b_high, b_low = halves(b)
    both = jnp.dot(jnp.concatenate([a_high, a_low], 0), b_high, preferred_element_type=F32)
    return both[:rows] + both[rows:] + jnp.dot(a_high, b_low, preferred_element_type=F32)


def apply_row(row, mat):
    return mm_apply(jnp.concatenate([row, row], 0), mat)[:8]


def mm_first(a, b):
    return lax.dot_general(
        a, b, (((0,), (0,)), ((), ())), precision=lax.Precision.HIGHEST, preferred_element_type=F32
    )


def eye(n):
    rows = lax.broadcasted_iota(jnp.int32, (n, n), 0)
    return rows == lax.broadcasted_iota(jnp.int32, (n, n), 1)


def column(row, n):
    return jnp.sum(jnp.where(eye(n), jnp.broadcast_to(row, (n, n)), 0.0), axis=1, keepdims=True)


def flip(place, bit):
    return place + bit * (1 - 2 * lax.rem(place // bit, 2))


def em_kernel(
    levels, obs_ref, flag_smem, flag_ref, trans_ref, map_ref, gain_ref, init_ref, cov_ref,
    smooth_ref, sums_ref,
    got_obs, table, push, flags, pad, send_map, got_map, send_vec, got_vec, sums, got_sums,
    held_tree, held_powers, send_sem, recv_sem,
):
    steps = push.shape[0]
    width = trans_ref.shape[0]
    chunks = steps // 4
    tm = lax.axis_index("tm")
    core = lax.axis_index("replay")
    place = tm * 2 + core
    last = 2**levels - 1

    def bit(k):
        return lax.rem(place // 2**k, 2)

    def target(mask):
        other = tm
        for k in range(1, levels):
            if mask >> k & 1:
                other = flip(other, 2 ** (k - 1))
        return (other, 1 - core if mask & 1 else core)

    stages = [(low, min(2, levels - low)) for low in range(0, levels, 2)]
    masks = sorted(
        {2**k for k in range(levels)} | {x << low for low, bits in stages for x in range(1, 2**bits)}
    )
    barrier = pltpu.get_barrier_semaphore()
    for mask in masks:
        pl.semaphore_signal(barrier, inc=1, device_id=target(mask), device_id_type=MESH)
    pl.semaphore_wait(barrier, len(masks))

    used = [0]

    def send(src, dst, mask):
        slot = used[0]
        used[0] += 1
        copy = pltpu.make_async_remote_copy(
            src_ref=src, dst_ref=dst, send_sem=send_sem.at[slot], recv_sem=recv_sem.at[slot],
            device_id=target(mask), device_id_type=MESH,
        )
        copy.start()
        return copy

    half = steps // 2
    away = pl.multiple_of((1 - core) * half, 8)
    near = pl.multiple_of(core * half, 8)
    obs_copy = send(obs_ref.at[0, pl.ds(away, half), :], got_obs, 1)

    trans = trans_ref[...]
    trans_t = trans.T
    scaled_map = map_ref[...] * column(gain_ref[...], gain_ref.shape[1])
    keep = jnp.where(eye(width), 1.0, 0.0) - mm_first(scaled_map, map_ref[...])
    corr_t = mm(trans_t, keep)
    back_t = mm(trans, keep)
    ones = [trans_t, corr_t]
    both = jnp.concatenate(ones, 1)
    twos = mm(jnp.concatenate(ones, 0), both)
    pairs = [twos[a * width:(a + 1) * width, b * width:(b + 1) * width] for a in range(2) for b in range(2)]
    wide = jnp.concatenate(pairs, 1)
    for a in range(4):
        fours = mm(pairs[a], wide)
        for b in range(4):
            table[a * 4 + b] = fours[:, b * width:(b + 1) * width]

    flags[...] = jnp.broadcast_to(column(flag_ref[...].astype(F32), steps), flags.shape)
    obs_copy.wait_recv()
    own_push = mm_apply(obs_ref[0, pl.ds(near, half), :], scaled_map)
    got_push = mm_apply(got_obs[...], scaled_map)
    push[pl.ds(0, half, stride=2), :] = jnp.where(core == 0, own_push, got_push)
    push[pl.ds(1, half, stride=2), :] = jnp.where(core == 0, got_push, own_push)

    step_flags = [flags[pl.ds(j, chunks, stride=4), :] for j in range(4)]
    step_push = [push[pl.ds(j, chunks, stride=4), :] * step_flags[j] for j in range(4)]

    def advance(state, j, times=mm):
        moved = times(state, both)
        return jnp.where(step_flags[j] > 0, moved[:, width:], moved[:, :width]) + step_push[j]

    state = step_push[0]
    for j in range(1, 4):
        state = advance(state, j, mm_apply)

    def quad(q):
        f = [flag_smem[4 * q + j] for j in range(4)]
        return table[f[0] * 8 + f[1] * 4 + f[2] * 2 + f[3]]

    def spread(row):
        return jnp.broadcast_to(row, (8, width))

    def compose(early, late):
        moved = mm(jnp.concatenate(early, 0), late[0])
        return (moved[:width], moved[width:] + late[1])

    placed = [0]

    def keep_node(mat, vec):
        at = placed[0]
        placed[0] += 1
        held_tree[at, :width] = mat
        held_tree[at, width:] = vec
        return at

    def node(at):
        return (held_tree[at, :width], held_tree[at, width:])

    tree = [[keep_node(quad(q), spread(state[q:q + 1])) for q in range(chunks)]]
    while len(tree[-1]) > 1:
        ids = tree[-1]
        tree.append(
            [keep_node(*compose(node(ids[i]), node(ids[i + 1]))) for i in range(0, len(ids), 2)]
        )
    total = node(tree[-1][0])

    held_powers[0] = back_t
    powers = {1: 0}

    def power(n):
        if n not in powers:
            low = n // 2 if n & (n - 1) == 0 else n & -n
            value = mm(power(low), power(n - low))
            powers[n] = len(powers)
            held_powers[powers[n]] = value
        return held_powers[powers[n]]

    ahead = [[1, 2, 3, 4], [8, 12, 16], [32, 48, 64], [128, 192, 256], [512, 768]]
    mix_t = mm(trans_t, back_t)
    copies = []
    before = None
    for k in range(levels):
        send_map[k, :width] = total[0]
        send_map[k, width:] = total[1]
        copies.append(send(send_map.at[k], got_map.at[k], 2**k))
        for n in ahead[k] if k < len(ahead) else []:
            power(n)
        if k == 1:
            before = (
                jnp.where(bit(0) == 1, got_map[0, :width], jnp.where(eye(width), 1.0, 0.0)),
                jnp.where(bit(0) == 1, got_map[0, width:], 0.0),
            )
        elif k > 1:
            longer = compose((got_map[k - 1, :width], got_map[k - 1, width:]), before)
            before = tuple(jnp.where(bit(k - 1) == 1, a, b) for a, b in zip(longer, before))
        copies[-1].wait_recv()
        if k < levels - 1:
            mine_late = bit(k) == 1
            got = (got_map[k, :width], got_map[k, width:])
            early = tuple(jnp.where(mine_late, a, b) for a, b in zip(got, total))
            late = tuple(jnp.where(mine_late, a, b) for a, b in zip(total, got))
            total = compose(early, late)
    begin = spread(init_ref[...])
    top = levels - 1
    begin = jnp.where(bit(top) == 1, mm(begin, got_map[top, :width]) + got_map[top, width:], begin)
    begin = mm(begin, before[0]) + before[1]

    heads = [begin]
    for ids in reversed(tree[:-1]):
        after = []
        for i, head in enumerate(heads):
            mat, vec = node(ids[2 * i])
            after.append(apply_row(head, mat) + vec)
        heads = [x for pair in zip(heads, after) for x in pair]
    lanes = lax.broadcasted_iota(jnp.int32, (8, width), 0)
    tiles = []
    for q in range(0, chunks, 8):
        tile = heads[q]
        for i in range(1, 8):
            tile = jnp.where(lanes == i, heads[q + i], tile)
        tiles.append(tile)
    state = jnp.concatenate(tiles, 0)
    for j in range(4):
        state = advance(state, j, mm_apply)
        push[pl.ds(j, chunks, stride=4), :] = state
    filtered = push[...]

    row_ids = lax.broadcasted_iota(jnp.int32, (steps, width), 0)
    final = jnp.logical_and(row_ids == steps - 1, place == last)
    blended = jnp.where(final, filtered, filtered - mm(filtered, mix_t))

    pad[steps:, :] = jnp.zeros((steps, width), F32)

    def suffixes(rows):
        stride = 1
        while stride < steps:
            pad[:steps, :] = rows
            moved = jnp.concatenate([pad[n * stride:n * stride + steps, :] for n in (1, 2, 3)], 1)
            rows = rows + mm_apply(moved, jnp.concatenate([power(n * stride) for n in (1, 2, 3)], 0))
            stride *= 4
        return rows

    partial = suffixes(blended)
    whole = spread(partial[:1])
    tails = []
    for at, (low, bits) in enumerate(stages):
        size = 2**bits
        mine = lax.rem(place // 2**low, size)
        send_vec[at] = whole
        sent = [
            send(send_vec.at[at], got_vec.at[at, x - 1], x << low) for x in range(1, size)
        ]
        copies += sent
        jumps = [power(n * steps * 2**low) for n in range(1, size)]
        onward = jnp.where(eye(width), 1.0, 0.0)
        for n in range(1, size):
            onward = jnp.where(mine == size - 1 - n, jumps[n - 1], onward)
        for copy in sent:
            copy.wait_recv()
        values = []
        for q in range(size):
            value = whole
            for x in range(1, size):
                other = mine
                for k in range(bits):
                    if x >> k & 1:
                        other = flip(other, 2**k)
                value = jnp.where(other == q, got_vec[at, x - 1], value)
            values.append(value)
        whole = values[0]
        for q in range(1, size):
            whole = whole + apply_row(values[q], jumps[q - 1])
        tail = jnp.zeros((8, width), F32)
        for q in reversed(range(1, size)):
            if q == size - 1:
                longer = values[q]
            else:
                longer = values[q] + apply_row(tail, jumps[0])
            tail = jnp.where(mine < q, longer, tail)
        tails.append((tail, onward))
    arriving = tails[-1][0]
    for tail, onward in reversed(tails[:-1]):
        arriving = tail + apply_row(arriving, onward)
    entry = jnp.where(row_ids == steps - 1, mm(arriving, back_t)[:1], 0.0)
    smoothed = partial + suffixes(entry)
    smooth_ref[...] = smoothed

    pad[:steps, :] = smoothed
    pad[steps:steps + 8, :] = arriving
    following = pad[1:steps + 1, :]
    counted = jnp.where(final, 0.0, smoothed)
    moments = mm_apply(counted.T, jnp.concatenate([smoothed, following], 1))
    sums[0] = moments[:, :width]
    sums[1] = moments[:, width:]
    copies.append(send(sums.at[1 - core], got_sums.at[0], 1))
    pair_count = F32(steps * (last + 1) - 1)
    lag_t = pair_count * lax.dot_general(
        back_t, cov_ref[...], (((0,), (1,)), ((), ())),
        precision=lax.Precision.HIGHEST, preferred_element_type=F32,
    )
    copies[-1].wait_recv()
    held = jnp.where(core == 0, moments[:, :width], moments[:, width:]) + got_sums[0]
    mid = width // 2
    parts = [held[:mid], held[mid:]]
    order = list(range(1, levels))
    turned = order[len(order) // 2:] + order[:len(order) // 2]
    for at, pair in enumerate(zip(order, turned), 1):
        sent = []
        for i, k in enumerate(pair):
            rows = pl.ds(i * mid, mid)
            sums[1 + at, rows, :] = parts[i]
            sent.append(send(sums.at[1 + at, rows, :], got_sums.at[at, rows, :], 2**k))
        copies += sent
        for i in range(2):
            sent[i].wait_recv()
            parts[i] = parts[i] + got_sums[at, i * mid:(i + 1) * mid, :]
    held = jnp.concatenate(parts, 0)
    sums[1 + levels] = held
    copies.append(send(sums.at[1 + levels], got_sums.at[levels], 1))
    copies[-1].wait_recv()
    other = got_sums[levels]
    sums_ref[:, :width] = jnp.where(core == 0, held, other) + pair_count * cov_ref[...]
    sums_ref[:, width:] = jnp.where(core == 0, other, held) + lag_t
    obs_copy.wait_send()
    for copy in copies:
        copy.wait_send()


def solve_kernel(sums_ref, smooth_ref, out_ref, smooth_out_ref):
    smooth_out_ref[...] = smooth_ref[...]
    width = out_ref.shape[0]
    groups = width // 8
    parts = [sums_ref[8 * g:8 * g + 8, :] for g in range(groups)]
    sub = lax.broadcasted_iota(jnp.int32, (8, 1), 0)
    for k in range(width):
        group, row = k // 8, k % 8
        pivot_row = parts[group][row:row + 1, :]
        scaled = pivot_row * (1.0 / pivot_row[:, k:k + 1])
        fresh = []
        for g in range(groups):
            reduced = parts[g] - parts[g][:, k:k + 1] * scaled
            if g == group:
                reduced = jnp.where(sub == row, scaled, reduced)
            fresh.append(reduced)
        parts = fresh
    out_ref[...] = jnp.concatenate([p[:, width:] for p in parts], 0).T


def local(levels, obs_store, observed, transition, obs_map, gain_weights, init_mean, smoothed_cov):
    steps = observed.shape[0]
    width = transition.shape[0]
    vmem = pl.BlockSpec(memory_space=pltpu.VMEM)
    smem = pl.BlockSpec(memory_space=pltpu.SMEM)
    copies = 1 + levels + 3 * (levels + 1) // 2 + 2 * levels + 2
    smoothed, sums = pl.pallas_call(
        functools.partial(em_kernel, levels),
        out_shape=(
            jax.ShapeDtypeStruct((steps, width), F32),
            jax.ShapeDtypeStruct((width, 2 * width), F32),
        ),
        in_specs=[vmem, smem, vmem, vmem, vmem, vmem, vmem, vmem],
        out_specs=(vmem, vmem),
        scratch_shapes=[
            pltpu.VMEM((steps // 2, obs_map.shape[0]), F32),
            pltpu.VMEM((16, width, width), F32),
            pltpu.VMEM((steps, width), F32),
            pltpu.VMEM((steps, width), F32),
            pltpu.VMEM((2 * steps, width), F32),
            pltpu.VMEM((levels, width + 8, width), F32),
            pltpu.VMEM((levels, width + 8, width), F32),
            pltpu.VMEM((levels, 8, width), F32),
            pltpu.VMEM((levels, 3, 8, width), F32),
            pltpu.VMEM((levels + 2, width, width), F32),
            pltpu.VMEM((levels + 1, width, width), F32),
            pltpu.VMEM((steps // 2 - 1, width + 8, width), F32),
            pltpu.VMEM((24, width, width), F32),
            pltpu.SemaphoreType.DMA((copies,)),
            pltpu.SemaphoreType.DMA((copies,)),
        ],
        compiler_params=pltpu.CompilerParams(collective_id=0, has_side_effects=True),
    )(
        obs_store, observed, observed.reshape(1, -1), transition, obs_map,
        gain_weights.reshape(1, -1), init_mean.reshape(1, -1), smoothed_cov,
    )
    new_transition, smoothed = pl.pallas_call(
        solve_kernel,
        out_shape=(
            jax.ShapeDtypeStruct((width, width), F32),
            jax.ShapeDtypeStruct((steps, width), F32),
        ),
        in_specs=[vmem, vmem],
        out_specs=(vmem, vmem),
    )(sums, smoothed)
    return (smoothed, new_transition)


def solution(mesh):
    levels = (mesh.shape["tm"] * mesh.shape["replay"]).bit_length() - 1
    return jax.shard_map(
        functools.partial(local, levels),
        mesh=mesh,
        in_specs=(P("replay", "tm", None), P(("tm", "replay")), P(), P(), P(), P(), P()),
        out_specs=(P(("tm", "replay"), None), P()),
        check_vma=False,
    )
```

profile of v0, /device:TPU:0, one launch (start us, length us, event | category | flops | bytes accessed | tf_op | source)
XLA Modules:
  0.0 69.5 jit_solution(16150503395734310449)
XLA Ops:
  0.6 56.3 %shard_map.86 = (f32[64,128]{1,0:T(8,128)}, f32[128,256]{1,0:T(8,128)}) custom-call(f32[1,64,64]{2,1,0:T(8,128)} %obs_ref.1, s32[64]{0:T(128)} %flag_smem.1, s32[1,64]{1,0:T(1,128)} %bitcast.3, f32[128,128]{1,0:T(8,128)} %trans_ref.1, f32[64,128]{1,0:T(8,128)} %map_ref.1, f32[1,64]{1,0:T(1,128)} %bitcast.4, f32[1,128]{1,0:T(1,128)} %bitcast.5, ...), custom_call_target="tpu_custom_call" | custom-call | tf_op jit(solution)/shard_map/pallas_call | solution.py:357
  56.9 12.6 %shard_map.87 = (f32[128,128]{1,0:T(8,128)}, f32[64,128]{1,0:T(8,128)}) custom-call(f32[128,256]{1,0:T(8,128)} %get-tuple-element.6.sums_ref, f32[64,128]{1,0:T(8,128)} %get-tuple-element.7.smooth_ref), custom_call_target="tpu_custom_call" | custom-call | tf_op jit(solution)/shard_map/pallas_call | solution.py:387
where the time goes:
time: 69.7 us; the launch traced here: 69.5 us
  Pallas kernels  68.9 us (99%)
    pallas_call x1, Pallas kernels, local(): pl.pallas_call(functools.partial(em_kernel, levels), out_shape=(jax.Shape...  56.3 us
    pallas_call x1, Pallas kernels, local(): pl.pallas_call(solve_kernel, out_shape=(jax.ShapeDtypeStruct((width, widt...  12.6 us

commit v1 on v0

--- a/solution.py
+++ b/solution.py
@@ -328,24 +328,90 @@
         copy.wait_send()
 
 
+def product(x, y):
+    return [
+        [sum((x[i][k] * y[k][j] for k in range(1, len(y))), x[i][0] * y[0][j]) for j in range(len(y[0]))]
+        for i in range(len(x))
+    ]
+
+
+def small_inverse(d):
+    n = len(d)
+    if n == 1:
+        return [[1.0 / d[0][0]]]
+    if n == 2:
+        det = 1.0 / (d[0][0] * d[1][1] - d[0][1] * d[0][1])
+        off = -d[0][1] * det
+        return [[d[1][1] * det, off], [off, d[0][0] * det]]
+    h = n // 2
+    head = small_inverse([r[:h] for r in d[:h]])
+    side = [r[h:] for r in d[:h]]
+    spread = product(head, side)
+    fill = product([list(x) for x in zip(*side)], spread)
+    rest = small_inverse([[d[h + i][h + j] - fill[i][j] for j in range(h)] for i in range(h)])
+    back = product(spread, rest)
+    fill = product(back, [list(x) for x in zip(*spread)])
+    top = [[head[i][j] + fill[i][j] for j in range(h)] + [-x for x in back[i]] for i in range(h)]
+    return top + [[-back[j][i] for j in range(h)] + rest[i] for i in range(h)]
+
+
+def combine(rows, weights):
+    total = rows[0] * weights[0]
+    for row, weight in zip(rows[1:], weights[1:]):
+        total = total + row * weight
+    return total
+
+
 def solve_kernel(sums_ref, smooth_ref, out_ref, smooth_out_ref):
     smooth_out_ref[...] = smooth_ref[...]
     width = out_ref.shape[0]
     groups = width // 8
-    parts = [sums_ref[8 * g:8 * g + 8, :] for g in range(groups)]
-    sub = lax.broadcasted_iota(jnp.int32, (8, 1), 0)
-    for k in range(width):
-        group, row = k // 8, k % 8
-        pivot_row = parts[group][row:row + 1, :]
-        scaled = pivot_row * (1.0 / pivot_row[:, k:k + 1])
-        fresh = []
-        for g in range(groups):
-            reduced = parts[g] - parts[g][:, k:k + 1] * scaled
-            if g == group:
-                reduced = jnp.where(sub == row, scaled, reduced)
-            fresh.append(reduced)
-        parts = fresh
-    out_ref[...] = jnp.concatenate([p[:, width:] for p in parts], 0).T
+    per = 4
+    full = (8, width)
+    left = [sums_ref[8 * g:8 * g + 8, :width] for g in range(groups)]
+    right = [sums_ref[8 * g:8 * g + 8, width:] for g in range(groups)]
+    lane = lax.broadcasted_iota(jnp.int32, (1, width), 1)
+    sub = lax.broadcasted_iota(jnp.int32, full, 0)
+
+    def spread_row(tile, i):
+        return jnp.broadcast_to(tile[i:i + 1, :], full)
+
+    for at in range(0, groups, per):
+        panel = range(at, at + per)
+        for pivot in panel:
+            cols = {
+                g: [jnp.broadcast_to(left[g][:, k:k + 1], full) for k in range(8 * pivot, 8 * pivot + 8)]
+                for g in panel
+            }
+            inverse = small_inverse(
+                [[spread_row(cols[pivot][max(i, j)], min(i, j)) for j in range(8)] for i in range(8)]
+            )
+            for side in (left, right):
+                rows = [spread_row(side[pivot], j) for j in range(8)]
+                solved = [combine(rows, inverse[i]) for i in range(8)]
+                for g in panel:
+                    if g == pivot:
+                        tile = solved[0]
+                        for j in range(1, 8):
+                            tile = jnp.where(sub == j, solved[j], tile)
+                        side[g] = tile
+                    else:
+                        side[g] = side[g] - combine(cols[g], solved)
+        mask = jnp.logical_and(lane >= 8 * at, lane < 8 * (at + per))
+        order = [g % groups for g in range(at + per, at + groups)]
+        rows = [jnp.concatenate([left[g], right[g]], 1) for g in panel]
+        before, after = 8 * at, 8 * (groups - at - per)
+        if before:
+            rows = [jnp.zeros((before, 2 * width), F32)] + rows
+        if after:
+            rows = rows + [jnp.zeros((after, 2 * width), F32)]
+        change = mm(
+            jnp.concatenate([jnp.where(mask, left[g], 0.0) for g in order], 0), jnp.concatenate(rows, 0)
+        )
+        for i, g in enumerate(order):
+            left[g] = left[g] - change[8 * i:8 * i + 8, :width]
+            right[g] = right[g] - change[8 * i:8 * i + 8, width:]
+    out_ref[...] = jnp.concatenate(right, 0).T
 
 
 def local(levels, obs_store, observed, transition, obs_map, gain_weights, init_mean, smoothed_cov):

time: 69.7 us -> 64.2 us (0.921)
  Pallas kernels: 68.9 us -> 63.4 us
    pallas_call x1, Pallas kernels: 12.6 us -> 7.14 us  [local(): pl.pallas_call(solve_kernel, out_shape=(jax.ShapeDtypeStruct((width, widt...]
where the time goes in v1:
time: 64.2 us; the launch traced here: 64.1 us
  Pallas kernels  63.4 us (99%)
    pallas_call x1, Pallas kernels, local(): pl.pallas_call(functools.partial(em_kernel, levels), out_shape=(jax.Shape...  56.3 us
    pallas_call x1, Pallas kernels, local(): pl.pallas_call(solve_kernel, out_shape=(jax.ShapeDtypeStruct((width, widt...  7.14 us

profile of v1, /device:TPU:0, one launch (start us, length us, event | category | flops | bytes accessed | tf_op | source)
XLA Modules:
  0.0 64.1 jit_solution(11714865911845015383)
XLA Ops:
  0.6 56.3 %shard_map.86 = (f32[64,128]{1,0:T(8,128)}, f32[128,256]{1,0:T(8,128)}) custom-call(f32[1,64,64]{2,1,0:T(8,128)} %obs_ref.1, s32[64]{0:T(128)} %flag_smem.1, s32[1,64]{1,0:T(1,128)} %bitcast.3, f32[128,128]{1,0:T(8,128)} %trans_ref.1, f32[64,128]{1,0:T(8,128)} %map_ref.1, f32[1,64]{1,0:T(1,128)} %bitcast.4, f32[1,128]{1,0:T(1,128)} %bitcast.5, ...), custom_call_target="tpu_custom_call" | custom-call | tf_op jit(solution)/shard_map/pallas_call | solution.py:423
  56.9 7.1 %shard_map.87 = (f32[128,128]{1,0:T(8,128)}, f32[64,128]{1,0:T(8,128)}) custom-call(f32[128,256]{1,0:T(8,128)} %get-tuple-element.6.sums_ref, f32[64,128]{1,0:T(8,128)} %get-tuple-element.7.smooth_ref), custom_call_target="tpu_custom_call" | custom-call | tf_op jit(solution)/shard_map/pallas_call | solution.py:453

commit v2 on v1

--- a/solution.py
+++ b/solution.py
@@ -28,6 +28,13 @@
     return both[:rows] + both[rows:] + jnp.dot(a_high, b_low, preferred_element_type=F32)
 
 
+def mm_halves(a, b_halves):
+    rows = a.shape[0]
+    a_high, a_low = halves(a)
+    both = jnp.dot(jnp.concatenate([a_high, a_low], 0), b_halves[0], preferred_element_type=F32)
+    return both[:rows] + both[rows:] + jnp.dot(a_high, b_halves[1], preferred_element_type=F32)
+
+
 def apply_row(row, mat):
     return mm_apply(jnp.concatenate([row, row], 0), mat)[:8]
 
@@ -54,8 +61,8 @@
 def em_kernel(
     levels, obs_ref, flag_smem, flag_ref, trans_ref, map_ref, gain_ref, init_ref, cov_ref,
     smooth_ref, sums_ref,
-    got_obs, table, push, flags, pad, send_map, got_map, send_vec, got_vec, sums, got_sums,
-    held_tree, held_powers, send_sem, recv_sem,
+    got_obs, table, push, flags, pad, own_map, core_map, chip_maps, got_start, next_start, got_tails,
+    moment, got_moment, line_moment, full_moment, held_tree, held_powers, send_sem, recv_sem,
 ):
     steps = push.shape[0]
     width = trans_ref.shape[0]
@@ -63,43 +70,48 @@
     tm = lax.axis_index("tm")
     core = lax.axis_index("replay")
     place = tm * 2 + core
-    last = 2**levels - 1
-
-    def bit(k):
-        return lax.rem(place // 2**k, 2)
-
-    def target(mask):
-        other = tm
-        for k in range(1, levels):
+    count = 2**levels
+    last = count - 1
+    near_bits = 3
+    mates = 2**near_bits
+    lines = count // mates
+    mine = lax.rem(place, mates)
+    line = place // mates
+
+    def at_place(other):
+        return (other // 2, lax.rem(other, 2))
+
+    def mate(mask):
+        other = place
+        for k in range(near_bits):
             if mask >> k & 1:
-                other = flip(other, 2 ** (k - 1))
-        return (other, 1 - core if mask & 1 else core)
-
-    stages = [(low, min(2, levels - low)) for low in range(0, levels, 2)]
-    masks = sorted(
-        {2**k for k in range(levels)} | {x << low for low, bits in stages for x in range(1, 2**bits)}
-    )
+                other = flip(other, 2**k)
+        return other
+
     barrier = pltpu.get_barrier_semaphore()
-    for mask in masks:
-        pl.semaphore_signal(barrier, inc=1, device_id=target(mask), device_id_type=MESH)
-    pl.semaphore_wait(barrier, len(masks))
+    for step in range(1, count):
+        pl.semaphore_signal(
+            barrier, inc=1, device_id=at_place(lax.rem(place + step, count)), device_id_type=MESH
+        )
 
     used = [0]
 
-    def send(src, dst, mask):
+    def remote(src, dst, other):
         slot = used[0]
         used[0] += 1
-        copy = pltpu.make_async_remote_copy(
+        return pltpu.make_async_remote_copy(
             src_ref=src, dst_ref=dst, send_sem=send_sem.at[slot], recv_sem=recv_sem.at[slot],
-            device_id=target(mask), device_id_type=MESH,
+            device_id=at_place(other), device_id_type=MESH,
         )
+
+    def send(src, dst, other):
+        copy = remote(src, dst, other)
         copy.start()
         return copy
 
     half = steps // 2
     away = pl.multiple_of((1 - core) * half, 8)
     near = pl.multiple_of(core * half, 8)
-    obs_copy = send(obs_ref.at[0, pl.ds(away, half), :], got_obs, 1)
 
     trans = trans_ref[...]
     trans_t = trans.T
@@ -117,6 +129,8 @@
         for b in range(4):
             table[a * 4 + b] = fours[:, b * width:(b + 1) * width]
 
+    pl.semaphore_wait(barrier, count - 1)
+    obs_copy = send(obs_ref.at[0, pl.ds(away, half), :], got_obs, mate(1))
     flags[...] = jnp.broadcast_to(column(flag_ref[...].astype(F32), steps), flags.shape)
     obs_copy.wait_recv()
     own_push = mm_apply(obs_ref[0, pl.ds(near, half), :], scaled_map)
@@ -177,35 +191,64 @@
             held_powers[powers[n]] = value
         return held_powers[powers[n]]
 
-    ahead = [[1, 2, 3, 4], [8, 12, 16], [32, 48, 64], [128, 192, 256], [512, 768]]
+    def read_map(ref):
+        return (ref[:width], ref[width:])
+
+    def pick(early, late, test):
+        return tuple(jnp.where(test, a, b) for a, b in zip(early, late))
+
+    def move(row, step_map):
+        return mm(row, step_map[0]) + step_map[1]
+
+    nothing = (jnp.where(eye(width), 1.0, 0.0), jnp.zeros((8, width), F32))
+    own_map[:width] = total[0]
+    own_map[width:] = total[1]
+    copies = [send(own_map, core_map, mate(1))]
     mix_t = mm(trans_t, back_t)
-    copies = []
-    before = None
-    for k in range(levels):
-        send_map[k, :width] = total[0]
-        send_map[k, width:] = total[1]
-        copies.append(send(send_map.at[k], got_map.at[k], 2**k))
-        for n in ahead[k] if k < len(ahead) else []:
-            power(n)
-        if k == 1:
-            before = (
-                jnp.where(bit(0) == 1, got_map[0, :width], jnp.where(eye(width), 1.0, 0.0)),
-                jnp.where(bit(0) == 1, got_map[0, width:], 0.0),
-            )
-        elif k > 1:
-            longer = compose((got_map[k - 1, :width], got_map[k - 1, width:]), before)
-            before = tuple(jnp.where(bit(k - 1) == 1, a, b) for a, b in zip(longer, before))
-        copies[-1].wait_recv()
-        if k < levels - 1:
-            mine_late = bit(k) == 1
-            got = (got_map[k, :width], got_map[k, width:])
-            early = tuple(jnp.where(mine_late, a, b) for a, b in zip(got, total))
-            late = tuple(jnp.where(mine_late, a, b) for a, b in zip(total, got))
-            total = compose(early, late)
-    begin = spread(init_ref[...])
-    top = levels - 1
-    begin = jnp.where(bit(top) == 1, mm(begin, got_map[top, :width]) + got_map[top, width:], begin)
-    begin = mm(begin, before[0]) + before[1]
+    for n in (1, 2, 3, 4, 8):
+        power(n)
+    copies[-1].wait_recv()
+    other_core = read_map(core_map)
+    total = compose(pick(total, other_core, core == 0), pick(other_core, total, core == 0))
+    chip = lax.rem(place // 2, 4)
+    chip_maps[chip, :width] = total[0]
+    chip_maps[chip, width:] = total[1]
+    sent = [send(chip_maps.at[chip], chip_maps.at[chip], mate(mask)) for mask in (6, 2, 4)]
+    copies += sent
+    for n in (12, 16, 32, 48, 64, 128, 256, 512):
+        power(n)
+    for copy in sent:
+        copy.wait_recv()
+    maps = [read_map(chip_maps.at[i]) for i in range(4)]
+    first_two = compose(maps[0], maps[1])
+    all_four = compose(first_two, compose(maps[2], maps[3]))
+    onward = remote(next_start, got_start, lax.rem(place + mates, count))
+
+    @pl.when(line == 0)
+    def _():
+        start = spread(init_ref[...])
+        got_start[...] = start
+        next_start[...] = move(start, all_four)
+        onward.start()
+
+    before = pick(compose(first_two, maps[2]), first_two, chip == 3)
+    before = pick(maps[0], before, chip == 1)
+    before = pick(nothing, before, chip == 0)
+    before = pick(compose(before, other_core), before, core == 1)
+    tail_tiles = count // 8
+    for n in list(range(1, 8)) + [8 * a for a in range(1, tail_tiles)]:
+        power(n * steps)
+
+    @pl.when(line > 0)
+    def _():
+        onward.wait_recv()
+
+    @pl.when(jnp.logical_and(line > 0, line < lines - 1))
+    def _():
+        next_start[...] = move(got_start[...], all_four)
+        onward.start()
+
+    begin = move(got_start[...], before)
 
     heads = [begin]
     for ids in reversed(tree[:-1]):
@@ -243,46 +286,24 @@
         return rows
 
     partial = suffixes(blended)
-    whole = spread(partial[:1])
-    tails = []
-    for at, (low, bits) in enumerate(stages):
-        size = 2**bits
-        mine = lax.rem(place // 2**low, size)
-        send_vec[at] = whole
-        sent = [
-            send(send_vec.at[at], got_vec.at[at, x - 1], x << low) for x in range(1, size)
-        ]
-        copies += sent
-        jumps = [power(n * steps * 2**low) for n in range(1, size)]
-        onward = jnp.where(eye(width), 1.0, 0.0)
-        for n in range(1, size):
-            onward = jnp.where(mine == size - 1 - n, jumps[n - 1], onward)
-        for copy in sent:
-            copy.wait_recv()
-        values = []
-        for q in range(size):
-            value = whole
-            for x in range(1, size):
-                other = mine
-                for k in range(bits):
-                    if x >> k & 1:
-                        other = flip(other, 2**k)
-                value = jnp.where(other == q, got_vec[at, x - 1], value)
-            values.append(value)
-        whole = values[0]
-        for q in range(1, size):
-            whole = whole + apply_row(values[q], jumps[q - 1])
-        tail = jnp.zeros((8, width), F32)
-        for q in reversed(range(1, size)):
-            if q == size - 1:
-                longer = values[q]
-            else:
-                longer = values[q] + apply_row(tail, jumps[0])
-            tail = jnp.where(mine < q, longer, tail)
-        tails.append((tail, onward))
-    arriving = tails[-1][0]
-    for tail, onward in reversed(tails[:-1]):
-        arriving = tail + apply_row(arriving, onward)
+    got_tails[last] = partial[:1]
+    sent = [
+        send(got_tails.at[last], got_tails.at[n], lax.rem(place + 2 * count - 1 - n, count))
+        for n in range(last)
+    ]
+    copies += sent
+    far = halves(jnp.concatenate([power(8 * a * steps) for a in range(1, tail_tiles)], 0))
+    close = halves(jnp.concatenate([power(n * steps) for n in range(1, 8)], 0))
+    for copy in sent:
+        copy.wait_recv()
+    order = lax.broadcasted_iota(jnp.int32, (count, width), 0)
+    later = jnp.where(order < last - place, got_tails[:, 0, :], 0.0)
+    folded = later[:8] + mm_halves(
+        jnp.concatenate([later[8 * a:8 * a + 8] for a in range(1, tail_tiles)], 1), far
+    )
+    arriving = spread(folded[:1]) + mm_halves(
+        jnp.concatenate([spread(folded[n:n + 1]) for n in range(1, 8)], 1), close
+    )
     entry = jnp.where(row_ids == steps - 1, mm(arriving, back_t)[:1], 0.0)
     smoothed = partial + suffixes(entry)
     smooth_ref[...] = smoothed
@@ -292,37 +313,51 @@
     following = pad[1:steps + 1, :]
     counted = jnp.where(final, 0.0, smoothed)
     moments = mm_apply(counted.T, jnp.concatenate([smoothed, following], 1))
-    sums[0] = moments[:, :width]
-    sums[1] = moments[:, width:]
-    copies.append(send(sums.at[1 - core], got_sums.at[0], 1))
+    owned = width // mates
+    for n in range(mates):
+        moment[n] = moments[n * owned:(n + 1) * owned]
+    sent = [
+        send(moment.at[lax.rem(mate(mask), mates)], got_moment.at[mask], mate(mask))
+        for mask in (6, 7, 2, 3, 4, 5, 1)
+    ]
+    copies += sent
     pair_count = F32(steps * (last + 1) - 1)
     lag_t = pair_count * lax.dot_general(
         back_t, cov_ref[...], (((0,), (1,)), ((), ())),
         precision=lax.Precision.HIGHEST, preferred_element_type=F32,
     )
-    copies[-1].wait_recv()
-    held = jnp.where(core == 0, moments[:, :width], moments[:, width:]) + got_sums[0]
-    mid = width // 2
-    parts = [held[:mid], held[mid:]]
-    order = list(range(1, levels))
-    turned = order[len(order) // 2:] + order[:len(order) // 2]
-    for at, pair in enumerate(zip(order, turned), 1):
-        sent = []
-        for i, k in enumerate(pair):
-            rows = pl.ds(i * mid, mid)
-            sums[1 + at, rows, :] = parts[i]
-            sent.append(send(sums.at[1 + at, rows, :], got_sums.at[at, rows, :], 2**k))
-        copies += sent
-        for i in range(2):
-            sent[i].wait_recv()
-            parts[i] = parts[i] + got_sums[at, i * mid:(i + 1) * mid, :]
-    held = jnp.concatenate(parts, 0)
-    sums[1 + levels] = held
-    copies.append(send(sums.at[1 + levels], got_sums.at[levels], 1))
-    copies[-1].wait_recv()
-    other = got_sums[levels]
-    sums_ref[:, :width] = jnp.where(core == 0, held, other) + pair_count * cov_ref[...]
-    sums_ref[:, width:] = jnp.where(core == 0, other, held) + lag_t
+    for copy in sent:
+        copy.wait_recv()
+    held = moment[mine]
+    for n in range(1, mates):
+        held = held + got_moment[n]
+    line_moment[line] = held
+    sent = [
+        send(line_moment.at[line], line_moment.at[line], lax.rem(place + mates * n, count))
+        for n in range(1, lines)
+    ]
+    copies += sent
+    for copy in sent:
+        copy.wait_recv()
+    held = line_moment[0]
+    for n in range(1, lines):
+        held = held + line_moment[n]
+    full_moment[mine] = held
+    sent = [
+        send(full_moment.at[mine], full_moment.at[mine], mate(mask)) for mask in (6, 7, 2, 3, 4, 5, 1)
+    ]
+    copies += sent
+    for copy in sent:
+        copy.wait_recv()
+    extra = jnp.concatenate([pair_count * cov_ref[...], lag_t], 1)
+    for n in range(mates):
+        rows = slice(n * owned, (n + 1) * owned)
+        sums_ref[rows, :] = full_moment[n] + extra[rows]
+
+    @pl.when(line < lines - 1)
+    def _():
+        onward.wait_send()
+
     obs_copy.wait_send()
     for copy in copies:
         copy.wait_send()
@@ -419,7 +454,11 @@
     width = transition.shape[0]
     vmem = pl.BlockSpec(memory_space=pltpu.VMEM)
     smem = pl.BlockSpec(memory_space=pltpu.SMEM)
-    copies = 1 + levels + 3 * (levels + 1) // 2 + 2 * levels + 2
+    count = 2**levels
+    mates = 8
+    copies = 1 + 1 + 3 + 1 + (count - 1) + 2 * (mates - 1) + (count // mates - 1)
+    chip_map = (width + 8, width)
+    owned = (width // mates, 2 * width)
     smoothed, sums = pl.pallas_call(
         functools.partial(em_kernel, levels),
         out_shape=(
@@ -434,14 +473,18 @@
             pltpu.VMEM((steps, width), F32),
             pltpu.VMEM((steps, width), F32),
             pltpu.VMEM((2 * steps, width), F32),
-            pltpu.VMEM((levels, width + 8, width), F32),
-            pltpu.VMEM((levels, width + 8, width), F32),
-            pltpu.VMEM((levels, 8, width), F32),
-            pltpu.VMEM((levels, 3, 8, width), F32),
-            pltpu.VMEM((levels + 2, width, width), F32),
-            pltpu.VMEM((levels + 1, width, width), F32),
+            pltpu.VMEM(chip_map, F32),
+            pltpu.VMEM(chip_map, F32),
+            pltpu.VMEM((4, *chip_map), F32),
+            pltpu.VMEM((8, width), F32),
+            pltpu.VMEM((8, width), F32),
+            pltpu.VMEM((count, 1, width), F32),
+            pltpu.VMEM((mates, *owned), F32),
+            pltpu.VMEM((mates, *owned), F32),
+            pltpu.VMEM((count // mates, *owned), F32),
+            pltpu.VMEM((mates, *owned), F32),
             pltpu.VMEM((steps // 2 - 1, width + 8, width), F32),
-            pltpu.VMEM((24, width, width), F32),
+            pltpu.VMEM((24 + count // 8, width, width), F32),
             pltpu.SemaphoreType.DMA((copies,)),
             pltpu.SemaphoreType.DMA((copies,)),
         ],

time: 64.2 us -> 54 us (0.84)
  Pallas kernels: 63.4 us -> 53.2 us
    pallas_call x1, Pallas kernels: 56.3 us -> 46 us  [local(): pl.pallas_call(functools.partial(em_kernel, levels), out_shape=(jax.Shape...]
where the time goes in v2:
time: 54 us; the launch traced here: 53.8 us
  Pallas kernels  53.2 us (99%)
  between operations  0.64 us (1%)
    pallas_call x1, Pallas kernels, local(): pl.pallas_call(functools.partial(em_kernel, levels), out_shape=(jax.Shape...  46 us
    pallas_call x1, Pallas kernels, local(): pl.pallas_call(solve_kernel, out_shape=(jax.ShapeDtypeStruct((width, widt...  7.14 us

profile of v2, /device:TPU:0, one launch (start us, length us, event | category | flops | bytes accessed | tf_op | source)
XLA Modules:
  0.0 53.8 jit_solution(13066379807979657547)
XLA Ops:
  0.6 46.0 %shard_map.86 = (f32[64,128]{1,0:T(8,128)}, f32[128,256]{1,0:T(8,128)}) custom-call(f32[1,64,64]{2,1,0:T(8,128)} %obs_ref.1, s32[64]{0:T(128)} %flag_smem.1, s32[1,64]{1,0:T(1,128)} %bitcast.3, f32[128,128]{1,0:T(8,128)} %trans_ref.1, f32[64,128]{1,0:T(8,128)} %map_ref.1, f32[1,64]{1,0:T(1,128)} %bitcast.4, f32[1,128]{1,0:T(1,128)} %bitcast.5, ...), custom_call_target="tpu_custom_call" | custom-call | tf_op jit(solution)/shard_map/pallas_call | solution.py:462
  46.7 7.1 %shard_map.87 = (f32[128,128]{1,0:T(8,128)}, f32[64,128]{1,0:T(8,128)}) custom-call(f32[128,256]{1,0:T(8,128)} %get-tuple-element.6.sums_ref, f32[64,128]{1,0:T(8,128)} %get-tuple-element.7.smooth_ref), custom_call_target="tpu_custom_call" | custom-call | tf_op jit(solution)/shard_map/pallas_call | solution.py:496

commit v3 on v2

--- a/solution.py
+++ b/solution.py
@@ -11,16 +11,36 @@
 F32 = jnp.float32
 
 
-def mm(a, b):
-    return jnp.dot(a, b, precision=lax.Precision.HIGHEST, preferred_element_type=F32)
-
-
 def halves(a):
     high = a.astype(jnp.bfloat16)
     return high, (a - high.astype(F32)).astype(jnp.bfloat16)
 
 
+def thirds(a):
+    high = a.astype(jnp.bfloat16)
+    rest = a - high.astype(F32)
+    mid = rest.astype(jnp.bfloat16)
+    return high, mid, (rest - mid.astype(F32)).astype(jnp.bfloat16)
+
+
+def mm(a, b):
+    width = b.shape[1]
+    a_high, a_mid, a_low = thirds(a)
+    b_high, b_mid, b_low = thirds(b)
+    row = jnp.concatenate([b_high, b_mid], 1)
+    large = jnp.dot(
+        jnp.concatenate([a_high, a_mid], 1), jnp.concatenate([row, row], 0), preferred_element_type=F32
+    )
+    small = jnp.dot(
+        jnp.concatenate([a_low, a_high], 1), jnp.concatenate([b_high, b_low], 0),
+        preferred_element_type=F32,
+    )
+    return large[:, :width] + (large[:, width:] + small)
+
+
 def mm_apply(a, b):
+    if a.shape[1] == 128:
+        return mm_packed(a, b)
     rows = a.shape[0]
     a_high, a_low = halves(a)
     b_high, b_low = halves(b)
@@ -28,6 +48,15 @@
     return both[:rows] + both[rows:] + jnp.dot(a_high, b_low, preferred_element_type=F32)
 
 
+def mm_packed(a, b):
+    width = b.shape[1]
+    b_high, b_low = halves(b)
+    lower = jnp.concatenate([b_high, jnp.zeros_like(b_low)], 1)
+    weights = jnp.concatenate([jnp.concatenate([b_high, b_low], 1), lower], 0)
+    out = jnp.dot(jnp.concatenate(halves(a), 1), weights, preferred_element_type=F32)
+    return out[:, :width] + out[:, width:]
+
+
 def mm_halves(a, b_halves):
     rows = a.shape[0]
     a_high, a_low = halves(a)
@@ -61,7 +90,8 @@
 def em_kernel(
     levels, obs_ref, flag_smem, flag_ref, trans_ref, map_ref, gain_ref, init_ref, cov_ref,
     smooth_ref, sums_ref,
-    got_obs, table, push, flags, pad, own_map, core_map, chip_maps, got_start, next_start, got_tails,
+    got_obs, table, push, flags, pad, own_map, core_map, chip_maps, got_start, next_start, got_near,
+    got_far, held_steps, held_jumps,
     moment, got_moment, line_moment, full_moment, held_tree, held_powers, send_sem, recv_sem,
 ):
     steps = push.shape[0]
@@ -88,11 +118,11 @@
                 other = flip(other, 2**k)
         return other
 
+    others = [mate(mask) for mask in range(1, mates)]
+    others += [lax.rem(place + mates * n, count) for n in range(1, lines)]
     barrier = pltpu.get_barrier_semaphore()
-    for step in range(1, count):
-        pl.semaphore_signal(
-            barrier, inc=1, device_id=at_place(lax.rem(place + step, count)), device_id_type=MESH
-        )
+    for other in others:
+        pl.semaphore_signal(barrier, inc=1, device_id=at_place(other), device_id_type=MESH)
 
     used = [0]
 
@@ -129,7 +159,7 @@
         for b in range(4):
             table[a * 4 + b] = fours[:, b * width:(b + 1) * width]
 
-    pl.semaphore_wait(barrier, count - 1)
+    pl.semaphore_wait(barrier, len(others))
     obs_copy = send(obs_ref.at[0, pl.ds(away, half), :], got_obs, mate(1))
     flags[...] = jnp.broadcast_to(column(flag_ref[...].astype(F32), steps), flags.shape)
     obs_copy.wait_recv()
@@ -157,7 +187,7 @@
         return jnp.broadcast_to(row, (8, width))
 
     def compose(early, late):
-        moved = mm(jnp.concatenate(early, 0), late[0])
+        moved = mm_packed(jnp.concatenate(early, 0), late[0])
         return (moved[:width], moved[width:] + late[1])
 
     placed = [0]
@@ -235,9 +265,16 @@
     before = pick(maps[0], before, chip == 1)
     before = pick(nothing, before, chip == 0)
     before = pick(compose(before, other_core), before, core == 1)
-    tail_tiles = count // 8
-    for n in list(range(1, 8)) + [8 * a for a in range(1, tail_tiles)]:
+    for n in list(range(1, mates)) + [mates * n for n in range(1, lines - 1)]:
         power(n * steps)
+    across = nothing[0]
+    for n in range(1, mates):
+        across = jnp.where(mine == mates - 1 - n, power(n * steps), across)
+    jumps = [across] + [mm(power(mates * n * steps), across) for n in range(1, lines - 1)]
+    for n, jump in enumerate(jumps):
+        held_jumps[n * width:(n + 1) * width] = jump
+    for n in range(1, mates):
+        held_steps[(n - 1) * width:n * width] = power(n * steps)
 
     @pl.when(line > 0)
     def _():
@@ -286,24 +323,33 @@
         return rows
 
     partial = suffixes(blended)
-    got_tails[last] = partial[:1]
+    got_near[mates:] = jnp.zeros((mates, 1, width), F32)
+    got_near[mine] = partial[:1]
+    sent = [send(got_near.at[mine], got_near.at[mine], mate(mask)) for mask in (6, 7, 2, 3, 4, 5, 1)]
+    copies += sent
+    steps_halves = halves(held_steps[...])
+    for copy in sent:
+        copy.wait_recv()
+    rows = [got_near[n] for n in range(mates)]
+    after = [got_near[mine + 1 + n] for n in range(mates)]
+    both_rows = jnp.concatenate(
+        [jnp.concatenate([spread(a), spread(b)], 0) for a, b in zip(rows[1:], after[1:])], 1
+    )
+    folded = mm_halves(both_rows, steps_halves)
+    got_far[lines - 1] = folded[:1] + rows[0]
+    tail = folded[8:] + spread(after[0])
     sent = [
-        send(got_tails.at[last], got_tails.at[n], lax.rem(place + 2 * count - 1 - n, count))
-        for n in range(last)
+        send(got_far.at[lines - 1], got_far.at[n], lax.rem(place + mates * (2 * lines - 1 - n), count))
+        for n in range(lines - 1)
     ]
     copies += sent
-    far = halves(jnp.concatenate([power(8 * a * steps) for a in range(1, tail_tiles)], 0))
-    close = halves(jnp.concatenate([power(n * steps) for n in range(1, 8)], 0))
+    jumps_halves = halves(held_jumps[...])
     for copy in sent:
         copy.wait_recv()
-    order = lax.broadcasted_iota(jnp.int32, (count, width), 0)
-    later = jnp.where(order < last - place, got_tails[:, 0, :], 0.0)
-    folded = later[:8] + mm_halves(
-        jnp.concatenate([later[8 * a:8 * a + 8] for a in range(1, tail_tiles)], 1), far
-    )
-    arriving = spread(folded[:1]) + mm_halves(
-        jnp.concatenate([spread(folded[n:n + 1]) for n in range(1, 8)], 1), close
-    )
+    later = [
+        jnp.where(n < lines - 1 - line, spread(got_far[n]), 0.0) for n in range(lines - 1)
+    ]
+    arriving = tail + mm_halves(jnp.concatenate(later, 1), jumps_halves)
     entry = jnp.where(row_ids == steps - 1, mm(arriving, back_t)[:1], 0.0)
     smoothed = partial + suffixes(entry)
     smooth_ref[...] = smoothed
@@ -456,7 +502,8 @@
     smem = pl.BlockSpec(memory_space=pltpu.SMEM)
     count = 2**levels
     mates = 8
-    copies = 1 + 1 + 3 + 1 + (count - 1) + 2 * (mates - 1) + (count // mates - 1)
+    lines = count // mates
+    copies = 6 + 3 * (mates - 1) + 2 * (lines - 1)
     chip_map = (width + 8, width)
     owned = (width // mates, 2 * width)
     smoothed, sums = pl.pallas_call(
@@ -478,13 +525,16 @@
             pltpu.VMEM((4, *chip_map), F32),
             pltpu.VMEM((8, width), F32),
             pltpu.VMEM((8, width), F32),
-            pltpu.VMEM((count, 1, width), F32),
+            pltpu.VMEM((2 * mates, 1, width), F32),
+            pltpu.VMEM((lines, 1, width), F32),
+            pltpu.VMEM(((mates - 1) * width, width), F32),
+            pltpu.VMEM(((lines - 1) * width, width), F32),
             pltpu.VMEM((mates, *owned), F32),
             pltpu.VMEM((mates, *owned), F32),
-            pltpu.VMEM((count // mates, *owned), F32),
+            pltpu.VMEM((lines, *owned), F32),
             pltpu.VMEM((mates, *owned), F32),
             pltpu.VMEM((steps // 2 - 1, width + 8, width), F32),
-            pltpu.VMEM((24 + count // 8, width, width), F32),
+            pltpu.VMEM((24 + lines, width, width), F32),
             pltpu.SemaphoreType.DMA((copies,)),
             pltpu.SemaphoreType.DMA((copies,)),
         ],

time: 54 us -> 51.5 us (0.954)
  Pallas kernels: 53.2 us -> 50.7 us
    pallas_call x1, Pallas kernels: 46 us -> 43.7 us  [local(): pl.pallas_call(functools.partial(em_kernel, levels), out_shape=(jax.Shape...]
where the time goes in v3:
time: 51.5 us; the launch traced here: 51.3 us
  Pallas kernels  50.7 us (98%)
  between operations  0.64 us (1%)
    pallas_call x1, Pallas kernels, local(): pl.pallas_call(functools.partial(em_kernel, levels), out_shape=(jax.Shape...  43.7 us
    pallas_call x1, Pallas kernels, local(): pl.pallas_call(solve_kernel, out_shape=(jax.ShapeDtypeStruct((width, widt...  6.98 us

profile of v3, /device:TPU:0, one launch (start us, length us, event | category | flops | bytes accessed | tf_op | source)
XLA Modules:
  0.0 51.3 jit_solution(3706998631837023106)
XLA Ops:
  0.6 43.7 %shard_map.86 = (f32[64,128]{1,0:T(8,128)}, f32[128,256]{1,0:T(8,128)}) custom-call(f32[1,64,64]{2,1,0:T(8,128)} %obs_ref.1, s32[64]{0:T(128)} %flag_smem.1, s32[1,64]{1,0:T(1,128)} %bitcast.3, f32[128,128]{1,0:T(8,128)} %trans_ref.1, f32[64,128]{1,0:T(8,128)} %map_ref.1, f32[1,64]{1,0:T(1,128)} %bitcast.4, f32[1,128]{1,0:T(1,128)} %bitcast.5, ...), custom_call_target="tpu_custom_call" | custom-call | tf_op jit(solution)/shard_map/pallas_call | solution.py:509
  44.3 7.0 %shard_map.87 = (f32[128,128]{1,0:T(8,128)}, f32[64,128]{1,0:T(8,128)}) custom-call(f32[128,256]{1,0:T(8,128)} %get-tuple-element.6.sums_ref, f32[64,128]{1,0:T(8,128)} %get-tuple-element.7.smooth_ref), custom_call_target="tpu_custom_call" | custom-call | tf_op jit(solution)/shard_map/pallas_call | solution.py:546

commit v4 on v3

--- a/solution.py
+++ b/solution.py
@@ -23,19 +23,22 @@
     return high, mid, (rest - mid.astype(F32)).astype(jnp.bfloat16)
 
 
+def weights_of(b):
+    high, mid, low = thirds(b)
+    row = jnp.concatenate([high, mid], 1)
+    return jnp.concatenate([row, row], 0), jnp.concatenate([high, low], 0)
+
+
+def mm_weights(a, weights):
+    width = weights[1].shape[1]
+    high, mid, low = thirds(a)
+    large = jnp.dot(jnp.concatenate([high, mid], 1), weights[0], preferred_element_type=F32)
+    small = jnp.dot(jnp.concatenate([low, high], 1), weights[1], preferred_element_type=F32)
+    return large[:, :width] + (large[:, width:] + small)
+
+
 def mm(a, b):
-    width = b.shape[1]
-    a_high, a_mid, a_low = thirds(a)
-    b_high, b_mid, b_low = thirds(b)
-    row = jnp.concatenate([b_high, b_mid], 1)
-    large = jnp.dot(
-        jnp.concatenate([a_high, a_mid], 1), jnp.concatenate([row, row], 0), preferred_element_type=F32
-    )
-    small = jnp.dot(
-        jnp.concatenate([a_low, a_high], 1), jnp.concatenate([b_high, b_low], 0),
-        preferred_element_type=F32,
-    )
-    return large[:, :width] + (large[:, width:] + small)
+    return mm_weights(a, weights_of(b))
 
 
 def mm_apply(a, b):
@@ -88,12 +91,23 @@
 
 
 def em_kernel(
-    levels, obs_ref, flag_smem, flag_ref, trans_ref, map_ref, gain_ref, init_ref, cov_ref,
+    levels, obs_in, flag_in, flag_row_in, trans_in, map_in, gain_in, init_in, cov_in,
     smooth_ref, sums_ref,
+    obs_ref, flag_smem, flag_ref, trans_ref, map_ref, gain_ref, init_ref, cov_ref, load_sem,
     got_obs, table, push, flags, pad, own_map, core_map, chip_maps, got_start, next_start, got_near,
     got_far, held_steps, held_jumps,
     moment, got_moment, line_moment, full_moment, held_tree, held_powers, send_sem, recv_sem,
 ):
+    pairs_in = [
+        (trans_in, trans_ref), (map_in, map_ref), (gain_in, gain_ref), (obs_in, obs_ref),
+        (flag_row_in, flag_ref), (flag_in, flag_smem), (init_in, init_ref), (cov_in, cov_ref),
+    ]
+    loads = [
+        pltpu.make_async_copy(source, place_ref, load_sem.at[i])
+        for i, (source, place_ref) in enumerate(pairs_in)
+    ]
+    for load in loads:
+        load.start()
     steps = push.shape[0]
     width = trans_ref.shape[0]
     chunks = steps // 4
@@ -143,6 +157,8 @@
     away = pl.multiple_of((1 - core) * half, 8)
     near = pl.multiple_of(core * half, 8)
 
+    for load in loads[:3]:
+        load.wait()
     trans = trans_ref[...]
     trans_t = trans.T
     scaled_map = map_ref[...] * column(gain_ref[...], gain_ref.shape[1])
@@ -159,6 +175,8 @@
         for b in range(4):
             table[a * 4 + b] = fours[:, b * width:(b + 1) * width]
 
+    for load in loads[3:]:
+        load.wait()
     pl.semaphore_wait(barrier, len(others))
     obs_copy = send(obs_ref.at[0, pl.ds(away, half), :], got_obs, mate(1))
     flags[...] = jnp.broadcast_to(column(flag_ref[...].astype(F32), steps), flags.shape)
@@ -226,9 +244,6 @@
 
     def pick(early, late, test):
         return tuple(jnp.where(test, a, b) for a, b in zip(early, late))
-
-    def move(row, step_map):
-        return mm(row, step_map[0]) + step_map[1]
 
     nothing = (jnp.where(eye(width), 1.0, 0.0), jnp.zeros((8, width), F32))
     own_map[:width] = total[0]
@@ -254,11 +269,14 @@
     all_four = compose(first_two, compose(maps[2], maps[3]))
     onward = remote(next_start, got_start, lax.rem(place + mates, count))
 
+    plane_weights = weights_of(all_four[0])
+    origin = spread(init_ref[...])
+    beyond = mm_weights(origin, plane_weights) + all_four[1]
+
     @pl.when(line == 0)
     def _():
-        start = spread(init_ref[...])
-        got_start[...] = start
-        next_start[...] = move(start, all_four)
+        got_start[...] = origin
+        next_start[...] = beyond
         onward.start()
 
     before = pick(compose(first_two, maps[2]), first_two, chip == 3)
@@ -276,16 +294,21 @@
     for n in range(1, mates):
         held_steps[(n - 1) * width:n * width] = power(n * steps)
 
+    before_weights = weights_of(before[0])
+
     @pl.when(line > 0)
     def _():
         onward.wait_recv()
 
+    start = got_start[...]
+    beyond = mm_weights(start, plane_weights) + all_four[1]
+
     @pl.when(jnp.logical_and(line > 0, line < lines - 1))
     def _():
-        next_start[...] = move(got_start[...], all_four)
+        next_start[...] = beyond
         onward.start()
 
-    begin = move(got_start[...], before)
+    begin = mm_weights(start, before_weights) + before[1]
 
     heads = [begin]
     for ids in reversed(tree[:-1]):
@@ -499,7 +522,6 @@
     steps = observed.shape[0]
     width = transition.shape[0]
     vmem = pl.BlockSpec(memory_space=pltpu.VMEM)
-    smem = pl.BlockSpec(memory_space=pltpu.SMEM)
     count = 2**levels
     mates = 8
     lines = count // mates
@@ -512,9 +534,18 @@
             jax.ShapeDtypeStruct((steps, width), F32),
             jax.ShapeDtypeStruct((width, 2 * width), F32),
         ),
-        in_specs=[vmem, smem, vmem, vmem, vmem, vmem, vmem, vmem],
+        in_specs=[pl.BlockSpec(memory_space=pltpu.HBM)] * 8,
         out_specs=(vmem, vmem),
         scratch_shapes=[
+            pltpu.VMEM(obs_store.shape, F32),
+            pltpu.SMEM((steps,), jnp.int32),
+            pltpu.VMEM((1, steps), jnp.int32),
+            pltpu.VMEM((width, width), F32),
+            pltpu.VMEM(obs_map.shape, F32),
+            pltpu.VMEM((1, obs_map.shape[0]), F32),
+            pltpu.VMEM((1, width), F32),
+            pltpu.VMEM((width, width), F32),
+            pltpu.SemaphoreType.DMA((8,)),
             pltpu.VMEM((steps // 2, obs_map.shape[0]), F32),
             pltpu.VMEM((16, width, width), F32),
             pltpu.VMEM((steps, width), F32),
@@ -538,11 +569,16 @@
             pltpu.SemaphoreType.DMA((copies,)),
             pltpu.SemaphoreType.DMA((copies,)),
         ],
-        compiler_params=pltpu.CompilerParams(collective_id=0, has_side_effects=True),
-    )(
-        obs_store, observed, observed.reshape(1, -1), transition, obs_map,
-        gain_weights.reshape(1, -1), init_mean.reshape(1, -1), smoothed_cov,
-    )
+        compiler_params=pltpu.CompilerParams(
+            collective_id=0, has_side_effects=True, vmem_limit_bytes=24 * 2**20
+        ),
+    )(*[
+        pltpu.with_memory_space_constraint(x, pltpu.HBM)
+        for x in (
+            obs_store, observed, observed.reshape(1, -1), transition, obs_map,
+            gain_weights.reshape(1, -1), init_mean.reshape(1, -1), smoothed_cov,
+        )
+    ])
     new_transition, smoothed = pl.pallas_call(
         solve_kernel,
         out_shape=(
@@ -551,6 +587,7 @@
         ),
         in_specs=[vmem, vmem],
         out_specs=(vmem, vmem),
+        compiler_params=pltpu.CompilerParams(vmem_limit_bytes=24 * 2**20),
     )(sums, smoothed)
     return (smoothed, new_transition)
 

time: 51.5 us -> 49.1 us (0.953)
  Pallas kernels: 50.7 us -> 48.3 us
    pallas_call x1, Pallas kernels: 43.7 us -> 42.3 us  [local(): pl.pallas_call(functools.partial(em_kernel, levels), out_shape=(jax.Shape...]
    pallas_call x1, Pallas kernels: 6.98 us -> 6.08 us  [local(): pl.pallas_call(solve_kernel, out_shape=(jax.ShapeDtypeStruct((width, widt...]
where the time goes in v4:
time: 49.1 us; the launch traced here: 49 us
  Pallas kernels  48.3 us (98%)
  between operations  0.64 us (1%)
    pallas_call x1, Pallas kernels, local(): pl.pallas_call(functools.partial(em_kernel, levels), out_shape=(jax.Shape...  42.3 us
    pallas_call x1, Pallas kernels, local(): pl.pallas_call(solve_kernel, out_shape=(jax.ShapeDtypeStruct((width, widt...  6.08 us

profile of v4, /device:TPU:0, one launch (start us, length us, event | category | flops | bytes accessed | tf_op | source)
XLA Modules:
  0.0 49.0 jit_solution(10235450919927378984)
XLA Ops:
  0.6 42.3 %shard_map.86 = (f32[64,128]{1,0:T(8,128)S(1)}, f32[128,256]{1,0:T(8,128)S(1)}) custom-call(f32[1,64,64]{2,1,0:T(8,128)} %obs_in.1, s32[64]{0:T(128)} %flag_in.1, s32[1,64]{1,0:T(1,128)} %bitcast.3, f32[128,128]{1,0:T(8,128)} %trans_in.1, f32[64,128]{1,0:T(8,128)} %map_in.1, f32[1,64]{1,0:T(1,128)} %bitcast.4, f32[1,128]{1,0:T(1,128)} %bitcast.5, ...), custom_call_target="tpu_custom_call" | custom-call | tf_op jit(solution)/shard_map/pallas_call | solution.py:531
  42.9 6.1 %shard_map.87 = (f32[128,128]{1,0:T(8,128)}, f32[64,128]{1,0:T(8,128)}) custom-call(f32[128,256]{1,0:T(8,128)S(1)} %get-tuple-element.6.sums_ref, f32[64,128]{1,0:T(8,128)S(1)} %get-tuple-element.7.smooth_ref), custom_call_target="tpu_custom_call" | custom-call | tf_op jit(solution)/shard_map/pallas_call | solution.py:582

commit v5 on v4

--- a/solution.py
+++ b/solution.py
@@ -94,7 +94,8 @@
     levels, obs_in, flag_in, flag_row_in, trans_in, map_in, gain_in, init_in, cov_in,
     smooth_ref, sums_ref,
     obs_ref, flag_smem, flag_ref, trans_ref, map_ref, gain_ref, init_ref, cov_ref, load_sem,
-    got_obs, table, push, flags, pad, own_map, core_map, chip_maps, got_start, next_start, got_near,
+    got_obs, table, push, flags, pad, own_map, core_map, chip_maps, got_start, next_start, got_leap, own_plane,
+    got_plane, got_near,
     got_far, held_steps, held_jumps,
     moment, got_moment, line_moment, full_moment, held_tree, held_powers, send_sem, recv_sem,
 ):
@@ -269,6 +270,20 @@
     all_four = compose(first_two, compose(maps[2], maps[3]))
     onward = remote(next_start, got_start, lax.rem(place + mates, count))
 
+    leap = remote(next_start, got_leap, lax.rem(place + 2 * mates, count))
+    lend = remote(own_plane, got_plane, lax.rem(place + mates, count))
+    odd = lax.rem(line, 2) == 1
+    lends = jnp.logical_and(jnp.logical_not(odd), jnp.logical_and(line > 0, line < lines - 1))
+    hands_on = jnp.logical_and(jnp.logical_or(odd, line == 0), line < lines - 1)
+    leaps = jnp.logical_and(odd, line < lines - 2)
+    borrows = jnp.logical_and(odd, line > 1)
+
+    @pl.when(lends)
+    def _():
+        own_plane[:width] = all_four[0]
+        own_plane[width:] = all_four[1]
+        lend.start()
+
     plane_weights = weights_of(all_four[0])
     origin = spread(init_ref[...])
     beyond = mm_weights(origin, plane_weights) + all_four[1]
@@ -296,17 +311,28 @@
 
     before_weights = weights_of(before[0])
 
-    @pl.when(line > 0)
+    @pl.when(borrows)
+    def _():
+        lend.wait_recv()
+        weights = weights_of(got_plane[:width])
+        leap.wait_recv()
+        got_start[...] = mm_weights(got_leap[...], weights) + got_plane[width:]
+
+    @pl.when(jnp.logical_and(line > 0, jnp.logical_not(borrows)))
     def _():
         onward.wait_recv()
 
     start = got_start[...]
     beyond = mm_weights(start, plane_weights) + all_four[1]
 
-    @pl.when(jnp.logical_and(line > 0, line < lines - 1))
+    @pl.when(jnp.logical_and(odd, line < lines - 1))
     def _():
         next_start[...] = beyond
         onward.start()
+
+    @pl.when(leaps)
+    def _():
+        leap.start()
 
     begin = mm_weights(start, before_weights) + before[1]
 
@@ -423,9 +449,17 @@
         rows = slice(n * owned, (n + 1) * owned)
         sums_ref[rows, :] = full_moment[n] + extra[rows]
 
-    @pl.when(line < lines - 1)
+    @pl.when(hands_on)
     def _():
         onward.wait_send()
+
+    @pl.when(leaps)
+    def _():
+        leap.wait_send()
+
+    @pl.when(lends)
+    def _():
+        lend.wait_send()
 
     obs_copy.wait_send()
     for copy in copies:
@@ -525,7 +559,7 @@
     count = 2**levels
     mates = 8
     lines = count // mates
-    copies = 6 + 3 * (mates - 1) + 2 * (lines - 1)
+    copies = 8 + 3 * (mates - 1) + 2 * (lines - 1)
     chip_map = (width + 8, width)
     owned = (width // mates, 2 * width)
     smoothed, sums = pl.pallas_call(
@@ -556,6 +590,9 @@
             pltpu.VMEM((4, *chip_map), F32),
             pltpu.VMEM((8, width), F32),
             pltpu.VMEM((8, width), F32),
+            pltpu.VMEM((8, width), F32),
+            pltpu.VMEM(chip_map, F32),
+            pltpu.VMEM(chip_map, F32),
             pltpu.VMEM((2 * mates, 1, width), F32),
             pltpu.VMEM((lines, 1, width), F32),
             pltpu.VMEM(((mates - 1) * width, width), F32),

time: 49.1 us -> 47.2 us (0.961)
  Pallas kernels: 48.3 us -> 46.4 us
    pallas_call x1, Pallas kernels: 42.3 us -> 40.4 us  [local(): pl.pallas_call(functools.partial(em_kernel, levels), out_shape=(jax.Shape...]
where the time goes in v5:
time: 47.2 us; the launch traced here: 47.1 us
  Pallas kernels  46.4 us (98%)
  between operations  0.64 us (1%)
    pallas_call x1, Pallas kernels, local(): pl.pallas_call(functools.partial(em_kernel, levels), out_shape=(jax.Shape...  40.4 us
    pallas_call x1, Pallas kernels, local(): pl.pallas_call(solve_kernel, out_shape=(jax.ShapeDtypeStruct((width, widt...  6.08 us

profile of v5, /device:TPU:0, one launch (start us, length us, event | category | flops | bytes accessed | tf_op | source)
XLA Modules:
  0.0 47.1 jit_solution(17763355281450073085)
XLA Ops:
  0.6 40.4 %shard_map.86 = (f32[64,128]{1,0:T(8,128)S(1)}, f32[128,256]{1,0:T(8,128)S(1)}) custom-call(f32[1,64,64]{2,1,0:T(8,128)} %obs_in.1, s32[64]{0:T(128)} %flag_in.1, s32[1,64]{1,0:T(1,128)} %bitcast.3, f32[128,128]{1,0:T(8,128)} %trans_in.1, f32[64,128]{1,0:T(8,128)} %map_in.1, f32[1,64]{1,0:T(1,128)} %bitcast.4, f32[1,128]{1,0:T(1,128)} %bitcast.5, ...), custom_call_target="tpu_custom_call" | custom-call | tf_op jit(solution)/shard_map/pallas_call | solution.py:565
  41.0 6.1 %shard_map.87 = (f32[128,128]{1,0:T(8,128)}, f32[64,128]{1,0:T(8,128)}) custom-call(f32[128,256]{1,0:T(8,128)S(1)} %get-tuple-element.6.sums_ref, f32[64,128]{1,0:T(8,128)S(1)} %get-tuple-element.7.smooth_ref), custom_call_target="tpu_custom_call" | custom-call | tf_op jit(solution)/shard_map/pallas_call | solution.py:619
